TPU v7x, 128 devices: a whole 4x4x4 slice. The times are simulated.
128 devices in a mesh: req: 16 (over y, x), tp: 8 (over z, core).
Axes of the slice: x: 4, y: 4, z: 4, core: 2. Of those that a mesh axis runs over, the one named last changes fastest.
Arguments:
- stream: bfloat16 [512, 2048], P('req'), may hold values from -1.5 to 1.5
- attn_gain: bfloat16 [2048], replicated, may hold values from 0.25 to 1.75
- mlp_gain: bfloat16 [2048], replicated, may hold values from 0.25 to 1.75
- w_query: bfloat16 [2048, 2048], P(None, 'tp'), may hold values from -0.125 to 0.125
- w_keyval: bfloat16 [2048, 2, 2048], P(None, None, 'tp'), may hold values from -30 to 30
- w_out: bfloat16 [2048, 2048], P('tp'), may hold values from -0.125 to 0.125
- w_gate_up: bfloat16 [2048, 2, 8192], P(None, None, 'tp'), may hold values from -0.125 to 0.125
- w_down: bfloat16 [8192, 2048], P('tp'), may hold values from -0.0625 to 0.0625
- root_cache: bfloat16 [8, 4096, 2, 2048], P(None, 'req', None, 'tp'), may hold values from -240 to 240
- mid_cache: bfloat16 [16, 2048, 2, 2048], P('req', None, None, 'tp'), may hold values from -240 to 240
- leaf_cache: bfloat16 [512, 128, 2, 2048], P('req', None, None, 'tp'), may hold values from -240 to 240
- held_hidden: bfloat16 [16, 256, 2048], P('req', None, 'tp'), may hold values from -6 to 6
- recompute_rows: int32 [16, 256], P('req'), may hold values from 0 to 2047, as said below
- root_len: int32 [8], replicated, may hold values from 1024 to 4096
- mid_len: int32 [16], replicated, may hold values from 256 to 2048
- leaf_len: int32 [512], P('req'), may hold values from 1 to 128
- mid_parent: int32 [16], replicated, may hold values from 0 to 7
- leaf_parent: int32 [512], replicated, may hold values from 0 to 15
Outputs:
- layer_out: bfloat16 [512, 2048], P('req', 'tp')
Inputs may be any that keep to these rules, and one draw needn't show every extreme that they name: `recompute_rows`: the 256 slots of one middle node are distinct.
All inputs are finite; a program needn't handle non-finite values.
Results may differ from a plain program's by a relative error of at most 0.02.
The roundings to bfloat16 on the way count: a program that leaves them out, or rounds other values in their place, can miss the bound.
Values may be sent and summed in bfloat16 or wider, within the bound.
A program may use at most 192 MiB of HBM per device.

v0:
```python
import math
import jax
import jax.numpy as jnp
from jax import lax
from jax.sharding import PartitionSpec as P

D = 2048
HEAD_DIM = 64
EPSILON = 1e-05
THETA_BASE = 130000.0
NEG_FILL = -1e30


def combined_all(value, axis, combine):
    everything = jax.tree.map(lambda part: lax.all_gather(part, axis), value)
    first = jax.tree.map(lambda part: part[0], everything)

    def lap(k, so_far):
        return combine(so_far, jax.tree.map(lambda part: part[k], everything))

    return lax.fori_loop(1, lax.axis_size(axis), lap, first)


def rms_scale(values, gain):
    return (
        values
        * lax.rsqrt(jnp.mean(values * values, axis=-1, keepdims=True) + EPSILON)
        * gain.astype(jnp.float32)
    )


def rotate(values, positions):
    half_dim = values.shape[-1] // 2
    inv_freq = jnp.exp(
        jnp.arange(half_dim, dtype=jnp.float32) * (-2.0 * math.log(THETA_BASE) / values.shape[-1])
    )
    angles = positions.astype(jnp.float32)[..., None, None] * inv_freq
    cosines = jnp.cos(angles)
    sines = jnp.sin(angles)
    leading = values[..., :half_dim]
    trailing = values[..., half_dim:]
    return jnp.concatenate(
        [leading * cosines - trailing * sines, trailing * cosines + leading * sines], axis=-1
    )


def lookup(table_values, indices):
    hits = indices[..., None] == jnp.arange(table_values.shape[0], dtype=jnp.int32)
    return jnp.sum(jnp.where(hits, table_values, 0), axis=-1)


def partial_softmax(queries, key_rows, live_mask, score_scale):
    count = key_rows.shape[0]
    heads = queries.shape[1]
    key_part = key_rows[:, 0].reshape(count, heads, HEAD_DIM)
    value_part = key_rows[:, 1].reshape(count, heads, HEAD_DIM)
    scores = (
        jnp.einsum("bhd,khd->hbk", queries, key_part, preferred_element_type=jnp.float32)
        * score_scale
    )
    live = live_mask[None]
    row_max = jnp.max(jnp.where(live, scores, NEG_FILL), axis=2)
    weights = jnp.where(live, jnp.exp(scores - row_max[..., None]), 0.0)
    row_sum = jnp.sum(weights, axis=2)
    weighted = jnp.einsum(
        "hbk,khd->bhd", weights.astype(jnp.bfloat16), value_part, preferred_element_type=jnp.float32
    )
    return (row_max.T, row_sum.T, weighted.reshape(queries.shape[0], heads * HEAD_DIM))


def join(earlier, latter):
    best = jnp.maximum(earlier[0], latter[0])
    factor_one = jnp.exp(earlier[0] - best)
    factor_two = jnp.exp(latter[0] - best)
    row_sum = earlier[1] * factor_one + latter[1] * factor_two
    weighted = earlier[2] * jnp.repeat(factor_one, HEAD_DIM, axis=1) + latter[2] * jnp.repeat(
        factor_two, HEAD_DIM, axis=1
    )
    return (best, row_sum, weighted)


def leaf_softmax(queries, leaf_cache, leaf_len, score_scale):
    own_rows, slots = leaf_cache.shape[:2]
    heads = queries.shape[1]
    key_part = leaf_cache[:, :, 0].reshape(own_rows, slots, heads, HEAD_DIM)
    value_part = leaf_cache[:, :, 1].reshape(own_rows, slots, heads, HEAD_DIM)
    scores = (
        jnp.einsum("rhd,rkhd->rhk", queries, key_part, preferred_element_type=jnp.float32)
        * score_scale
    )
    live = (jnp.arange(slots, dtype=jnp.int32)[None, :] < leaf_len[:, None])[:, None, :]
    row_max = jnp.max(jnp.where(live, scores, NEG_FILL), axis=2)
    weights = jnp.where(live, jnp.exp(scores - row_max[..., None]), 0.0)
    row_sum = jnp.sum(weights, axis=2)
    weighted = jnp.einsum(
        "rhk,rkhd->rhd",
        weights.astype(jnp.bfloat16),
        value_part,
        preferred_element_type=jnp.float32,
    )
    return (row_max, row_sum, weighted)


def on_device(
    stream,
    attn_gain,
    mlp_gain,
    w_query,
    w_keyval,
    w_out,
    w_gate_up,
    w_down,
    root_cache,
    mid_cache,
    leaf_cache,
    held_hidden,
    recompute_rows,
    root_len,
    mid_len,
    leaf_len,
    mid_parent,
    leaf_parent,
):
    req_rank = lax.axis_index("req")
    own_rows = stream.shape[0]
    query_width = w_query.shape[1]
    local_heads = query_width // HEAD_DIM
    score_scale = HEAD_DIM ** (-0.5)
    requests = leaf_parent.shape[0]
    all_roots = lookup(mid_parent, leaf_parent)
    own_mids = lax.dynamic_slice_in_dim(leaf_parent, req_rank * own_rows, own_rows)
    own_roots = lax.dynamic_slice_in_dim(all_roots, req_rank * own_rows, own_rows)
    positions = lookup(root_len, own_roots) + lookup(mid_len, own_mids) + leaf_len
    stream_float = stream.astype(jnp.float32)
    normed = rms_scale(stream_float, attn_gain).astype(jnp.bfloat16)
    keyval_flat = w_keyval.reshape(D, 2 * query_width)
    queries = rotate(
        jnp.dot(normed, w_query, preferred_element_type=jnp.float32).reshape(
            own_rows, local_heads, HEAD_DIM
        ),
        positions,
    ).astype(jnp.bfloat16)
    fresh = jnp.dot(normed, keyval_flat, preferred_element_type=jnp.float32).reshape(
        own_rows, 2, local_heads, HEAD_DIM
    )
    key_new = rotate(fresh[:, 0], positions).astype(jnp.bfloat16)
    value_new = fresh[:, 1].astype(jnp.bfloat16)
    node_count, slots = mid_cache.shape[:2]
    recomp_count = recompute_rows.shape[1]
    held = lax.all_gather(held_hidden, "tp", axis=2, tiled=True)
    held_normed = rms_scale(held.astype(jnp.float32), attn_gain).astype(jnp.bfloat16)
    rebuilt = jnp.dot(
        held_normed.reshape(node_count * recomp_count, D),
        keyval_flat,
        preferred_element_type=jnp.float32,
    ).reshape(node_count, recomp_count, 2, local_heads, HEAD_DIM)
    own_nodes = req_rank * node_count + jnp.arange(node_count, dtype=jnp.int32)
    own_lens = lax.dynamic_slice_in_dim(mid_len, req_rank * node_count, node_count)
    own_parents = lax.dynamic_slice_in_dim(mid_parent, req_rank * node_count, node_count)
    rebuilt_pos = lookup(root_len, own_parents)[:, None] + recompute_rows
    rebuilt = (
        jnp.stack([rotate(rebuilt[:, :, 0], rebuilt_pos), rebuilt[:, :, 1]], axis=2)
        .astype(jnp.bfloat16)
        .reshape(node_count * recomp_count, 2, query_width)
    )
    all_queries = lax.all_gather(
        queries.reshape(own_rows, query_width), "req", axis=0, tiled=True
    ).reshape(requests, local_heads, HEAD_DIM)
    root_count, slice_len = root_cache.shape[:2]
    token_ids = req_rank * slice_len + jnp.arange(slice_len, dtype=jnp.int32)
    root_valid = token_ids[None, :] < root_len[:, None]
    root_match = all_roots[:, None] == jnp.arange(root_count, dtype=jnp.int32)[None, :]
    root_mask = (root_match[:, :, None] & root_valid[None]).reshape(
        requests, root_count * slice_len
    )
    root_part = partial_softmax(
        all_queries,
        root_cache.reshape(root_count * slice_len, 2, query_width),
        root_mask,
        score_scale,
    )
    replaced = jnp.any(
        recompute_rows[:, :, None] == jnp.arange(slots, dtype=jnp.int32)[None, None, :], axis=1
    )
    slot_live = (jnp.arange(slots, dtype=jnp.int32)[None, :] < own_lens[:, None]) & jnp.logical_not(
        replaced
    )
    belongs = leaf_parent[:, None] == own_nodes[None, :]
    held_mask = (belongs[:, :, None] & slot_live[None]).reshape(requests, node_count * slots)
    fresh_mask = (belongs[:, :, None] & (recompute_rows < own_lens[:, None])[None]).reshape(
        requests, node_count * recomp_count
    )
    mid_keys = jnp.concatenate(
        [mid_cache.reshape(node_count * slots, 2, query_width), rebuilt], axis=0
    )
    mid_part = partial_softmax(
        all_queries, mid_keys, jnp.concatenate([held_mask, fresh_mask], axis=1), score_scale
    )
    part_max, part_sum, part_acc = join(root_part, mid_part)
    merged_max, merged_sum, merged_acc = combined_all((part_max, part_sum, part_acc), "req", join)
    remote_max = lax.dynamic_slice_in_dim(merged_max, req_rank * own_rows, own_rows, 0)[None]
    remote_sum = lax.dynamic_slice_in_dim(merged_sum, req_rank * own_rows, own_rows, 0)[None]
    remote_acc = lax.dynamic_slice_in_dim(merged_acc, req_rank * own_rows, own_rows, 0)[None]
    leaf_max, leaf_sum, leaf_acc = leaf_softmax(queries, leaf_cache, leaf_len, score_scale)
    self_score = (
        jnp.sum(queries.astype(jnp.float32) * key_new.astype(jnp.float32), axis=-1) * score_scale
    )
    best = jnp.maximum(jnp.maximum(jnp.max(remote_max, axis=0), leaf_max), self_score)
    remote_factor = jnp.exp(remote_max - best[None])
    leaf_factor = jnp.exp(leaf_max - best)
    self_factor = jnp.exp(self_score - best)
    row_sum = jnp.sum(remote_sum * remote_factor, axis=0) + leaf_sum * leaf_factor + self_factor
    sources = remote_acc.shape[0]
    weighted = jnp.sum(
        remote_acc.reshape(sources, own_rows, local_heads, HEAD_DIM) * remote_factor[..., None],
        axis=0,
    )
    weighted = (
        weighted
        + leaf_acc * leaf_factor[..., None]
        + value_new.astype(jnp.float32) * self_factor[..., None]
    )
    attended = (weighted / row_sum[..., None]).reshape(own_rows, query_width).astype(jnp.bfloat16)
    attn_part = jnp.dot(attended, w_out, preferred_element_type=jnp.float32)
    width_share = D // lax.axis_size("tp")
    tp_rank = lax.axis_index("tp")
    residual = stream_float + lax.psum(attn_part, "tp")
    mixed_in = rms_scale(residual, mlp_gain).astype(jnp.bfloat16)
    residual_share = lax.dynamic_slice_in_dim(residual, tp_rank * width_share, width_share, 1)
    hidden_width = w_gate_up.shape[2]
    projected = jnp.dot(
        mixed_in, w_gate_up.reshape(D, 2 * hidden_width), preferred_element_type=jnp.float32
    ).reshape(own_rows, 2, hidden_width)
    hidden = (jax.nn.silu(projected[:, 0]) * projected[:, 1]).astype(jnp.bfloat16)
    down_share = lax.psum_scatter(
        jnp.dot(hidden, w_down, preferred_element_type=jnp.float32),
        "tp",
        scatter_dimension=1,
        tiled=True,
    )
    return (residual_share + down_share).astype(jnp.bfloat16)


def solution(mesh):
    placed = (
        P("req", None),
        P(),
        P(),
        P(None, "tp"),
        P(None, None, "tp"),
        P("tp", None),
        P(None, None, "tp"),
        P("tp", None),
        P(None, "req", None, "tp"),
        P("req", None, None, "tp"),
        P("req", None, None, "tp"),
        P("req", None, "tp"),
        P("req", None),
        P(),
        P(),
        P("req"),
        P(),
        P(),
    )
    return jax.shard_map(
        on_device, mesh=mesh, in_specs=placed, out_specs=P("req", "tp"), check_vma=False
    )
```

profile of v0, /device:TPU:0, one launch (start us, length us, event | category | flops | bytes accessed | tf_op | source)
XLA Modules:
  0.0 369.5 jit_solution(2306715656610677094)
XLA Ops:
  16.6 2.1 copy.109
  18.7 2.5 copy.77
  21.2 2.8 fusion.44
  26.2 24.1 %all_gather.22 = bf16[512,256]{1,0:T(8,128)(2,1)S(1)} all-gather(bf16[32,256]{1,0:T(8,128)(2,1)S(1)} %convert_element_type.81), channel_id=1, replica_groups=mesh['req'=16,'tp'=8] {'req'}, dimensions={0}, use_global_device_ids=true | all-gather | bytes 278528 | tf_op jit(solution)/shard_map/all_gather | solution.py:166
  54.6 4.2 %fusion.81 = (bf16[2048,1,256]{2,1,0:T(2,128)(2,1)}, bf16[2048,1,256]{2,1,0:T(2,128)(2,1)}) fusion(bf16[2048,2,256]{2,1,0:T(2,128)(2,1)S(1)} %bitcast.183), kind=kLoop, calls=%fused_computation.143 | loop fusion | bytes 4194304 | tf_op jit(solution)/shard_map/slice | solution.py:56
  58.8 6.0 %copy.103 = bf16[2048,1,256]{0,2,1:T(8,128)(2,1)} copy(bf16[2048,1,256]{2,1,0:T(2,128)(2,1)} %get-tuple-element.234) | data formatting | bytes 2097152
  71.6 4.3 %copy.104 = bf16[2048,1,256]{0,2,1:T(8,128)(2,1)} copy(bf16[2048,1,256]{2,1,0:T(2,128)(2,1)S(1)} %copy-done.4) | data formatting | bytes 2097152
  77.9 2.5 pad_add_fusion
  80.3 4.5 %select_reduce_fusion.1 = (f32[4,512]{1,0:T(4,128)S(1)}, f32[4,512,2048]{2,1,0:T(8,128)S(1)}) fusion(pred[512,2048]{1,0:T(8,128)(4,1)S(1)} %broadcast_and_fusion.1, bf16[512,4,64]{0,2,1:T(8,128)(2,1)} %bitcast.189, bf16[2048,4,64]{0,2,1:T(8,128)(2,1)S(1)} %bitcast.188), kind=kOutput, calls=%fused_computation.13 | convolution fusion | flops 549451776 | bytes 19144704 | tf_op jit(solution)/shard_map/bhd,khd->hbk/dot_general | solution.py:58
  84.9 5.7 %copy-done.1 = f32[4,512,2048]{2,1,0:T(8,128)} copy-done((f32[4,512,2048]{2,1,0:T(8,128)}, f32[4,512,2048]{2,1,0:T(8,128)S(1)}, u32[]{:S(2)}) %copy-start.1) | copy-done | bytes 16777240
  90.6 5.2 %fusion.6 = f32[4,512]{1,0:T(4,128)} fusion(f32[4,512,2048]{2,1,0:T(8,128)S(1)} %get-tuple-element.253, f32[4,512]{1,0:T(4,128)S(1)} %get-tuple-element.252, pred[512,2048]{1,0:T(8,128)(4,1)S(1)} %broadcast_and_fusion.1), kind=kLoop, calls=%fused_computation.17 | loop fusion | flops 16775168 | bytes 17842176 | tf_op jit(solution)/shard_map/reduce_sum | solution.py:64
  97.3 2.8 convolution_bitcast_fusion
  100.6 13.3 %maximum_maximum_fusion = bf16[2304,2,256]{2,1,0:T(2,128)(2,1)S(1)} fusion(bf16[256,1,256]{2,1,0:T(2,128)(2,1)S(1)} %copy.79, bf16[256,1,256]{2,1,0:T(2,128)(2,1)S(1)} %copy.78, bf16[2048,2,256]{2,1,0:T(2,128)(2,1)} %bitcast.196), kind=kLoop, calls=%fused_computation.25 | loop fusion | flops 7077888 | bytes 4718592 | tf_op jit(solution)/shard_map/concatenate | solution.py:193
  113.9 4.8 %fusion.80 = (bf16[2304,1,256]{2,1,0:T(2,128)(2,1)}, bf16[2304,1,256]{2,1,0:T(2,128)(2,1)}) fusion(bf16[2304,2,256]{2,1,0:T(2,128)(2,1)S(1)} %maximum_maximum_fusion), kind=kLoop, calls=%fused_computation.142 | loop fusion | bytes 4718592 | tf_op jit(solution)/shard_map/slice | solution.py:56
  118.7 6.0 %copy.80 = bf16[2304,1,256]{0,2,1:T(8,128)(2,1)} copy(bf16[2304,1,256]{2,1,0:T(2,128)(2,1)} %get-tuple-element.232) | data formatting | bytes 2359296 | tf_op jit(solution)/shard_map/slice | solution.py:55
  124.7 6.0 %copy.82 = bf16[2304,1,256]{0,2,1:T(8,128)(2,1)} copy(bf16[2304,1,256]{2,1,0:T(2,128)(2,1)} %get-tuple-element.231) | data formatting | bytes 2359296 | tf_op jit(solution)/shard_map/slice | solution.py:56
  130.7 5.6 %select_reduce_fusion = (f32[4,512]{1,0:T(4,128)S(1)}, f32[4,512,2304]{2,1,0:T(8,128)S(1)}) fusion(pred[512,2304]{1,0:T(8,128)(4,1)} %pad_add_fusion, bf16[512,4,64]{0,2,1:T(8,128)(2,1)} %bitcast.190, bf16[2304,4,64]{0,2,1:T(8,128)(2,1)} %bitcast.187), kind=kOutput, calls=%fused_computation.11 | convolution fusion | flops 618133504 | bytes 21504000 | tf_op jit(solution)/shard_map/bhd,khd->hbk/dot_general | solution.py:58
  136.4 5.1 %fusion.4 = f32[4,512]{1,0:T(4,128)S(1)} fusion(f32[4,512,2304]{2,1,0:T(8,128)S(1)} %get-tuple-element.251, f32[4,512]{1,0:T(4,128)S(1)} %get-tuple-element.250, pred[512,2304]{1,0:T(8,128)(4,1)S(1)} %copy-done.2), kind=kLoop, calls=%fused_computation.15 | loop fusion | flops 18872320 | bytes 20070400 | tf_op jit(solution)/shard_map/reduce_sum | solution.py:64
  142.1 6.8 %fusion.29 = f32[512,4,64]{0,2,1:T(8,128)} fusion(bf16[2304,4,64]{0,2,1:T(8,128)(2,1)} %bitcast.197, f32[4,512,2304]{2,1,0:T(8,128)S(1)} %get-tuple-element.251, f32[4,512]{1,0:T(4,128)S(1)} %get-tuple-element.250, pred[512,2304]{1,0:T(8,128)(4,1)} %pad_add_fusion, f32[512,4]{0,1:T(4,128)} %get-tuple-element.228), kind=kOutput, calls=%fused_computation.38 | convolution fusion | flops 622985216 | bytes 21774336 | tf_op jit(solution)/shard_map/hbk,khd->bhd/dot_general | solution.py:65
  148.9 8.0 %fusion.26 = f32[512,4,64]{0,2,1:T(8,128)S(1)} fusion(f32[512,4,64]{0,2,1:T(8,128)} %fusion.29, bf16[2048,4,64]{0,2,1:T(8,128)(2,1)} %bitcast.198, f32[4,512,2048]{2,1,0:T(8,128)} %copy-done.1, f32[4,512]{1,0:T(4,128)S(1)} %copy-done.14, pred[512,2048]{1,0:T(8,128)(4,1)S(1)} %broadcast_and_fusion.1, f32[512,4]{0,1:T(4,128)S(1)} %get-tuple-element.227), kind=kOutput, calls=%fused_computation.37 | convolution fusion | flops 553910272 | bytes 19939328 | tf_op jit(solution)/shard_map/hbk,khd->bhd/dot_general | solution.py:65
  158.0 10.0 %fusion.79 = (bf16[32,128,1,256]{3,2,1,0:T(2,128)(2,1)}, bf16[32,128,1,256]{3,2,1,0:T(2,128)(2,1)}) fusion(bf16[32,128,2,256]{3,2,1,0:T(2,128)(2,1)} %param.30), kind=kLoop, calls=%fused_computation.141 | loop fusion | bytes 8388608 | tf_op jit(solution)/shard_map/slice | solution.py:85
  168.0 9.8 %copy.105 = bf16[32,128,1,256]{1,3,0,2:T(8,128)(2,1)} copy(bf16[32,128,1,256]{3,2,1,0:T(2,128)(2,1)} %get-tuple-element.229) | data formatting | bytes 4194304
  177.8 8.6 %copy.106 = bf16[32,128,1,256]{1,3,0,2:T(8,128)(2,1)S(1)} copy(bf16[32,128,1,256]{3,2,1,0:T(2,128)(2,1)} %get-tuple-element.230) | data formatting | bytes 4194304
  186.5 2.2 fusion.56
  190.2 23.4 %all-gather = f32[8192,4]{0,1:T(4,128)S(1)} all-gather(f32[512,4]{0,1:T(4,128)S(1)} %get-tuple-element.245), channel_id=2, replica_groups=mesh['req'=16,'tp'=8] {'req'}, dimensions={0}, use_global_device_ids=true | all-gather | bytes 139264 | tf_op jit(solution)/shard_map/all_gather | solution.py:15
  213.6 21.6 %all-gather.1 = f32[8192,4]{0,1:T(4,128)S(1)} all-gather(f32[512,4]{0,1:T(4,128)S(1)} %get-tuple-element.226), channel_id=3, replica_groups=mesh['req'=16,'tp'=8] {'req'}, dimensions={0}, use_global_device_ids=true | all-gather | bytes 139264 | tf_op jit(solution)/shard_map/all_gather | solution.py:15
  236.5 23.7 %while.19 = (s32[]{:T(128)}, f32[512,4]{0,1:T(4,128)S(1)}, f32[512,4]{0,1:T(4,128)S(1)}, f32[512,256]{0,1:T(8,128)S(1)}, f32[16,512,4]{1,2,0:T(4,128)S(1)}, /*in...) while((s32[]{:T(128)}, f32[512,4]{0,1:T(4,128)S(1)}, ...), condition=%wide.region_12.13_spmd, body=%wide.region_11.12_spmd.sunk | while | flops 405509 | bytes 3752087 | solution.py:21
  262.7 10.1 %copy.110 = bf16[256,8,2,1024]{3,1,2,0:T(8,128)(2,1)} copy(bf16[256,8,2,1024]{3,2,1,0:T(2,128)(2,1)} %bitcast.182) | data formatting | bytes 16777216
  272.8 12.4 %copy.91 = bf16[2048,2048]{1,0:T(8,128)(2,1)} copy(bf16[2048,2048]{0,1:T(8,128)(2,1)} %bitcast.181) | data formatting | bytes 16777216 | tf_op jit(solution)/shard_map/dot_general | solution.py:231
  285.2 37.8 %all-reduce.2.cloned.1.call-done = f32[32,2048]{1,0:T(8,128)} async-done(((f32[32,2048]{1,0:T(8,128)}), f32[32,2048]{1,0:T(8,128)}) %all-reduce.2.cloned.1.call-update) | async-done | bytes 262160 | tf_op jit(solution)/shard_map/psum | solution.py:227
  324.1 6.1 %fusion.40 = f32[32,2,1024]{2,0,1:T(8,128)S(1)} fusion(bf16[2,1024,2048]{2,1,0:T(8,128)(2,1)} %bitcast.180, f32[32,2048]{1,0:T(8,128)S(1)} %get-tuple-element.219, f32[2048]{0:T(1024)S(1)} %convert_element_type.94, f32[32]{0:T(128)S(1)} %add_rsqrt_fusion.1), kind=kOutput, calls=%fused_computation.56 | convolution fusion | flops 268632064 | bytes 8921216 | tf_op jit(solution)/shard_map/dot_general | solution.py:231
  331.8 29.8 %reduce-scatter.2.cloned.1.call-done = f32[32,256]{1,0:T(8,128)} async-done(((f32[32,2048]{1,0:T(8,128)}), f32[32,256]{1,0:T(8,128)}) %reduce-scatter.2.cloned.1.call-update) | async-done | bytes 32784 | tf_op jit(solution)/shard_map/reduce_scatter | solution.py:235
  (184 shorter events, 61.3 us)
Async XLA Ops:
  6.5 255.1 %copy-start = (bf16[256,2048]{1,0:T(8,128)(2,1)S(1)}, bf16[256,2048]{1,0:T(8,128)(2,1)}, u32[]{:S(2)}) copy-start(bf16[256,2048]{1,0:T(8,128)(2,1)} %param.25) | copy-start | bytes 3145732
  6.5 89.2 %all-gather.5.cloned.1.call-start = ((), (), s32[]{:S(2)}) async-start(), calls=%async_computation.1 | async-start | bytes 1179648 | tf_op jit(solution)/shard_map/all_gather | solution.py:150
  7.3 228.0 %all-gather.7.cloned.1.call-start = ((), (), s32[]{:S(2)}) async-start(), calls=%async_computation.2 | async-start | bytes 8912896 | tf_op jit(solution)/shard_map/all_gather | solution.py:15
  16.6 4.6 %copy-start.7 = (bf16[32,2048]{1,0:T(8,128)(2,1)S(1)}, bf16[32,2048]{1,0:T(8,128)(2,1)}, u32[]{:S(2)}) copy-start(bf16[32,2048]{1,0:T(8,128)(2,1)} %param.20) | copy-start | bytes 393220
  18.7 5.4 %copy-start.21 = (s32[8]{0:T(128)S(1)}, s32[8]{0:T(128)}, u32[]{:S(2)}) copy-start(s32[8]{0:T(128)} %param.33) | copy-start | bytes 100
  18.7 5.5 %copy-start.19 = (s32[32]{0:T(128)S(1)}, s32[32]{0:T(128)}, u32[]{:S(2)}) copy-start(s32[32]{0:T(128)} %param.35) | copy-start | bytes 388
  21.2 33.4 %copy-start.3 = (bf16[8,256,2,256]{3,2,1,0:T(2,128)(2,1)S(1)}, bf16[8,256,2,256]{3,2,1,0:T(2,128)(2,1)}, u32[]{:S(2)}) copy-start(bf16[8,256,2,256]{3,2,1,0:T(2,128)(2,1)} %param.28) | copy-start | bytes 6291460
  24.1 0.7 copy-start.9
  25.5 0.6 copy-start.11
  54.6 11.5 %copy-start.18 = (s32[1,256]{1,0:T(1,128)S(1)}, s32[1,256]{1,0:T(1,128)}, u32[]{:S(2)}) copy-start(s32[1,256]{1,0:T(1,128)} %param.32) | copy-start | bytes 3076
  58.8 12.8 %copy-start.4 = (bf16[2048,1,256]{2,1,0:T(2,128)(2,1)S(1)}, bf16[2048,1,256]{2,1,0:T(2,128)(2,1)}, u32[]{:S(2)}) copy-start(bf16[2048,1,256]{2,1,0:T(2,128)(2,1)} %get-tuple-element.233) | copy-start | bytes 3145732
  75.9 4.5 %copy-start.5 = (bf16[2048,1,256]{0,2,1:T(8,128)(2,1)S(1)}, bf16[2048,1,256]{0,2,1:T(8,128)(2,1)}, u32[]{:S(2)}) copy-start(bf16[2048,1,256]{0,2,1:T(8,128)(2,1)} %copy.103) | copy-start | bytes 3145732
  84.9 5.7 %copy-start.1 = (f32[4,512,2048]{2,1,0:T(8,128)}, f32[4,512,2048]{2,1,0:T(8,128)S(1)}, u32[]{:S(2)}) copy-start(f32[4,512,2048]{2,1,0:T(8,128)S(1)} %get-tuple-element.253) | copy-start | bytes 50331652
  84.9 5.7 %copy-start.13 = (f32[4,512]{1,0:T(4,128)}, f32[4,512]{1,0:T(4,128)S(1)}, u32[]{:S(2)}) copy-start(f32[4,512]{1,0:T(4,128)S(1)} %get-tuple-element.252) | copy-start | bytes 24580
  95.8 4.3 %copy-start.10 = (f32[256,32]{0,1:T(8,128)S(1)}, f32[256,32]{0,1:T(8,128)}, u32[]{:S(2)}) copy-start(f32[256,32]{0,1:T(8,128)} %get-tuple-element.247) | copy-start | bytes 98308
  130.7 5.6 %copy-start.2 = (pred[512,2304]{1,0:T(8,128)(4,1)S(1)}, pred[512,2304]{1,0:T(8,128)(4,1)}, u32[]{:S(2)}) copy-start(pred[512,2304]{1,0:T(8,128)(4,1)} %pad_add_fusion) | copy-start | bytes 3538948
  136.4 5.1 %copy-start.14 = (f32[4,512]{1,0:T(4,128)S(1)}, f32[4,512]{1,0:T(4,128)}, u32[]{:S(2)}) copy-start(f32[4,512]{1,0:T(4,128)} %copy-done.13) | copy-start | bytes 24580
  136.4 5.1 %copy-start.15 = (f32[4,512]{1,0:T(4,128)S(1)}, f32[4,512]{1,0:T(4,128)}, u32[]{:S(2)}) copy-start(f32[4,512]{1,0:T(4,128)} %fusion.6) | copy-start | bytes 24580
  157.9 165.1 %all-reduce.2.cloned.1.call-start = ((), (), s32[]{:S(2)}) async-start(), calls=%async_computation.3 | async-start | bytes 524288 | tf_op jit(solution)/shard_map/psum | solution.py:227
  177.8 8.6 %copy-start.20 = (s32[32]{0:T(128)S(1)}, s32[32]{0:T(128)}, u32[]{:S(2)}) copy-start(s32[32]{0:T(128)} %param.35) | copy-start | bytes 388
  177.8 8.7 %copy-start.12 = (bf16[32,4,64]{2,0,1:T(8,128)(2,1)S(1)}, bf16[32,4,64]{2,0,1:T(8,128)(2,1)}, u32[]{:S(2)}) copy-start(bf16[32,4,64]{2,0,1:T(8,128)(2,1)} %copy-done.11) | copy-start | bytes 49156
  236.5 23.9 %copy-start.16 = (f32[32,4]{0,1:T(4,128)S(1)}, f32[32,4]{0,1:T(4,128)}, u32[]{:S(2)}) copy-start(f32[32,4]{0,1:T(4,128)} %get-tuple-element.224) | copy-start | bytes 1540
  262.6 99.0 %reduce-scatter.2.cloned.1.call-start = ((), (), s32[]{:S(2)}) async-start(), calls=%async_computation.4 | async-start | bytes 294912 | tf_op jit(solution)/shard_map/reduce_scatter | solution.py:235
  272.8 12.4 %copy-start.17 = (bf16[2048]{0:T(1024)(128)(2,1)S(1)}, bf16[2048]{0:T(1024)(128)(2,1)}, u32[]{:S(2)}) copy-start(bf16[2048]{0:T(1024)(128)(2,1)} %param.22) | copy-start | bytes 12292
  272.8 50.2 %copy-start.8 = (bf16[32,2048]{1,0:T(8,128)(2,1)S(1)}, bf16[32,2048]{1,0:T(8,128)(2,1)}, u32[]{:S(2)}) copy-start(bf16[32,2048]{1,0:T(8,128)(2,1)} %param.20) | copy-start | bytes 393220
  324.1 6.2 %copy-start.6 = (bf16[1024,2048]{1,0:T(8,128)(2,1)S(1)}, bf16[1024,2048]{1,0:T(8,128)(2,1)}, u32[]{:S(2)}) copy-start(bf16[1024,2048]{1,0:T(8,128)(2,1)} %param.27) | copy-start | bytes 12582916
Sparse Core Ops, SparseCore 0:
  9.0 26.0 all-gather.4
  158.0 71.9 all-gather.6
  262.7 60.1 all-reduce.1
  331.9 29.6 reduce-scatter.1
where the time goes:
time: 372 us; the launch traced here: 370 us
  local copies, waits for them, and re-layouts  124 us (33%)
  blocking collectives  69.1 us (19%)
  waiting for transfers between devices  68.4 us (18%)
  other arithmetic  50 us (13%)
  matrix products  44.2 us (12%)
  between operations  13.5 us (4%)
    unnamed x53, local copies, waits for them, and re-layouts  49.1 us
    all_gather x2, blocking collectives, combined_all(): everything = jax.tree.map(lambda part: lax.all_gather(part, axis), value)  45 us
    psum x1, waiting for transfers between devices, on_device(): residual = stream_float + lax.psum(attn_part, 'tp')  37.8 us
    reduce_scatter x1, waiting for transfers between devices, on_device(): lax.psum_scatter(jnp.dot(hidden, w_down, preferred_element_type=jnp.float...  29.8 us
    all_gather x1, blocking collectives, on_device(): lax.all_gather(queries.reshape(own_rows, query_width), 'req', axis=0, til...  24.1 us
    dynamic_slice x30, local copies, waits for them, and re-layouts, lap(): return combine(so_far, jax.tree.map(lambda part: part[k], everything))  19.2 us
    slice x3, local copies, waits for them, and re-layouts, partial_softmax(): value_part = key_rows[:, 1].reshape(count, heads, HEAD_DIM)  15 us
    dot_general x2, matrix products, partial_softmax(): jnp.einsum('hbk,khd->bhd', weights.astype(jnp.bfloat16), value_part, pref...  14.8 us
  transfers between devices with their start and end apart: 4, of which 2 were waited for; matrix products, arithmetic and copies ran while one was open for 30% of the time, Pallas kernels for 0%

commit v1 on v0

--- a/solution.py
+++ b/solution.py
@@ -224,7 +224,12 @@
     attn_part = jnp.dot(attended, w_out, preferred_element_type=jnp.float32)
     width_share = D // lax.axis_size("tp")
     tp_rank = lax.axis_index("tp")
-    residual = stream_float + lax.psum(attn_part, "tp")
+
+    def detail_floor_in(mine_x, row_axis):
+        vec_out = lax.all_gather(mine_x, row_axis)
+        return jnp.sum(vec_out, axis=0)
+
+    residual = stream_float + detail_floor_in(attn_part, "tp")
     mixed_in = rms_scale(residual, mlp_gain).astype(jnp.bfloat16)
     residual_share = lax.dynamic_slice_in_dim(residual, tp_rank * width_share, width_share, 1)
     hidden_width = w_gate_up.shape[2]

time: 372 us -> 340 us (0.914)
  waiting for transfers between devices: 68.4 us -> 35.1 us
    psum x1 -> x0, waiting for transfers between devices: 37.8 us -> none  [on_device(): residual = stream_float + lax.psum(attn_part, 'tp')]
  transfers between devices with their start and end apart: 4 -> 4, of which waited for: 2 -> 2; matrix products, arithmetic and copies ran while one was open for 30% -> 33% of each run, Pallas kernels for 0% -> 0%
where the time goes in v1:
time: 340 us; the launch traced here: 337 us
  local copies, waits for them, and re-layouts  124 us (36%)
  blocking collectives  69.1 us (20%)
  other arithmetic  50.8 us (15%)
  matrix products  44.2 us (13%)
  waiting for transfers between devices  35.1 us (10%)
  between operations  13.6 us (4%)
    unnamed x53, local copies, waits for them, and re-layouts  49.1 us
    all_gather x2, blocking collectives, combined_all(): everything = jax.tree.map(lambda part: lax.all_gather(part, axis), value)  45 us
    reduce_scatter x1, waiting for transfers between devices, on_device(): lax.psum_scatter(jnp.dot(hidden, w_down, preferred_element_type=jnp.float...  31.3 us
    all_gather x1, blocking collectives, on_device(): lax.all_gather(queries.reshape(own_rows, query_width), 'req', axis=0, til...  24.1 us
    dynamic_slice x30, local copies, waits for them, and re-layouts, lap(): return combine(so_far, jax.tree.map(lambda part: part[k], everything))  19.2 us
    slice x3, local copies, waits for them, and re-layouts, partial_softmax(): value_part = key_rows[:, 1].reshape(count, heads, HEAD_DIM)  15 us
    dot_general x2, matrix products, partial_softmax(): jnp.einsum('hbk,khd->bhd', weights.astype(jnp.bfloat16), value_part, pref...  14.8 us
    concatenate x1, other arithmetic, on_device(): jnp.concatenate([mid_cache.reshape(node_count * slots, 2, query_width), r...  13.3 us
  transfers between devices with their start and end apart: 4, of which 2 were waited for; matrix products, arithmetic and copies ran while one was open for 33% of the time, Pallas kernels for 0%

profile of v1, /device:TPU:0, one launch (start us, length us, event | category | flops | bytes accessed | tf_op | source)
XLA Modules:
  0.0 337.1 jit_solution(5786178928298028482)
XLA Ops:
  16.6 2.1 copy.109
  18.7 2.5 copy.77
  21.2 2.8 fusion.44
  26.2 24.1 %all_gather.28 = bf16[512,256]{1,0:T(8,128)(2,1)S(1)} all-gather(bf16[32,256]{1,0:T(8,128)(2,1)S(1)} %convert_element_type.81), channel_id=1, replica_groups=mesh['req'=16,'tp'=8] {'req'}, dimensions={0}, use_global_device_ids=true | all-gather | bytes 278528 | tf_op jit(solution)/shard_map/all_gather | solution.py:166
  54.6 4.2 %fusion.81 = (bf16[2048,1,256]{2,1,0:T(2,128)(2,1)}, bf16[2048,1,256]{2,1,0:T(2,128)(2,1)}) fusion(bf16[2048,2,256]{2,1,0:T(2,128)(2,1)S(1)} %bitcast.184), kind=kLoop, calls=%fused_computation.143 | loop fusion | bytes 4194304 | tf_op jit(solution)/shard_map/slice | solution.py:56
  58.8 6.0 %copy.103 = bf16[2048,1,256]{0,2,1:T(8,128)(2,1)} copy(bf16[2048,1,256]{2,1,0:T(2,128)(2,1)} %get-tuple-element.234) | data formatting | bytes 2097152
  71.6 4.3 %copy.104 = bf16[2048,1,256]{0,2,1:T(8,128)(2,1)} copy(bf16[2048,1,256]{2,1,0:T(2,128)(2,1)S(1)} %copy-done.4) | data formatting | bytes 2097152
  77.9 2.5 pad_add_fusion
  80.3 4.5 %select_reduce_fusion.1 = (f32[4,512]{1,0:T(4,128)S(1)}, f32[4,512,2048]{2,1,0:T(8,128)S(1)}) fusion(pred[512,2048]{1,0:T(8,128)(4,1)S(1)} %broadcast_and_fusion.1, bf16[512,4,64]{0,2,1:T(8,128)(2,1)} %bitcast.190, bf16[2048,4,64]{0,2,1:T(8,128)(2,1)S(1)} %bitcast.189), kind=kOutput, calls=%fused_computation.13 | convolution fusion | flops 549451776 | bytes 19144704 | tf_op jit(solution)/shard_map/bhd,khd->hbk/dot_general | solution.py:58
  84.9 5.7 %copy-done.1 = f32[4,512,2048]{2,1,0:T(8,128)} copy-done((f32[4,512,2048]{2,1,0:T(8,128)}, f32[4,512,2048]{2,1,0:T(8,128)S(1)}, u32[]{:S(2)}) %copy-start.1) | copy-done | bytes 16777240
  90.6 5.2 %fusion.6 = f32[4,512]{1,0:T(4,128)} fusion(f32[4,512,2048]{2,1,0:T(8,128)S(1)} %get-tuple-element.253, f32[4,512]{1,0:T(4,128)S(1)} %get-tuple-element.252, pred[512,2048]{1,0:T(8,128)(4,1)S(1)} %broadcast_and_fusion.1), kind=kLoop, calls=%fused_computation.17 | loop fusion | flops 16775168 | bytes 17842176 | tf_op jit(solution)/shard_map/reduce_sum | solution.py:64
  97.3 2.8 convolution_bitcast_fusion
  100.6 13.3 %maximum_maximum_fusion = bf16[2304,2,256]{2,1,0:T(2,128)(2,1)S(1)} fusion(bf16[256,1,256]{2,1,0:T(2,128)(2,1)S(1)} %copy.79, bf16[256,1,256]{2,1,0:T(2,128)(2,1)S(1)} %copy.78, bf16[2048,2,256]{2,1,0:T(2,128)(2,1)} %bitcast.198), kind=kLoop, calls=%fused_computation.25 | loop fusion | flops 7077888 | bytes 4718592 | tf_op jit(solution)/shard_map/concatenate | solution.py:193
  113.9 4.8 %fusion.80 = (bf16[2304,1,256]{2,1,0:T(2,128)(2,1)}, bf16[2304,1,256]{2,1,0:T(2,128)(2,1)}) fusion(bf16[2304,2,256]{2,1,0:T(2,128)(2,1)S(1)} %maximum_maximum_fusion), kind=kLoop, calls=%fused_computation.142 | loop fusion | bytes 4718592 | tf_op jit(solution)/shard_map/slice | solution.py:56
  118.7 6.0 %copy.80 = bf16[2304,1,256]{0,2,1:T(8,128)(2,1)} copy(bf16[2304,1,256]{2,1,0:T(2,128)(2,1)} %get-tuple-element.232) | data formatting | bytes 2359296 | tf_op jit(solution)/shard_map/slice | solution.py:55
  124.7 6.0 %copy.82 = bf16[2304,1,256]{0,2,1:T(8,128)(2,1)} copy(bf16[2304,1,256]{2,1,0:T(2,128)(2,1)} %get-tuple-element.231) | data formatting | bytes 2359296 | tf_op jit(solution)/shard_map/slice | solution.py:56
  130.7 5.6 %select_reduce_fusion = (f32[4,512]{1,0:T(4,128)S(1)}, f32[4,512,2304]{2,1,0:T(8,128)S(1)}) fusion(pred[512,2304]{1,0:T(8,128)(4,1)} %pad_add_fusion, bf16[512,4,64]{0,2,1:T(8,128)(2,1)} %bitcast.191, bf16[2304,4,64]{0,2,1:T(8,128)(2,1)} %bitcast.188), kind=kOutput, calls=%fused_computation.11 | convolution fusion | flops 618133504 | bytes 21504000 | tf_op jit(solution)/shard_map/bhd,khd->hbk/dot_general | solution.py:58
  136.4 5.1 %fusion.4 = f32[4,512]{1,0:T(4,128)S(1)} fusion(f32[4,512,2304]{2,1,0:T(8,128)S(1)} %get-tuple-element.251, f32[4,512]{1,0:T(4,128)S(1)} %get-tuple-element.250, pred[512,2304]{1,0:T(8,128)(4,1)S(1)} %copy-done.2), kind=kLoop, calls=%fused_computation.15 | loop fusion | flops 18872320 | bytes 20070400 | tf_op jit(solution)/shard_map/reduce_sum | solution.py:64
  142.1 6.8 %fusion.29 = f32[512,4,64]{0,2,1:T(8,128)} fusion(bf16[2304,4,64]{0,2,1:T(8,128)(2,1)} %bitcast.199, f32[4,512,2304]{2,1,0:T(8,128)S(1)} %get-tuple-element.251, f32[4,512]{1,0:T(4,128)S(1)} %get-tuple-element.250, pred[512,2304]{1,0:T(8,128)(4,1)} %pad_add_fusion, f32[512,4]{0,1:T(4,128)} %get-tuple-element.228), kind=kOutput, calls=%fused_computation.38 | convolution fusion | flops 622985216 | bytes 21774336 | tf_op jit(solution)/shard_map/hbk,khd->bhd/dot_general | solution.py:65
  148.9 8.0 %fusion.26 = f32[512,4,64]{0,2,1:T(8,128)S(1)} fusion(f32[512,4,64]{0,2,1:T(8,128)} %fusion.29, bf16[2048,4,64]{0,2,1:T(8,128)(2,1)} %bitcast.200, f32[4,512,2048]{2,1,0:T(8,128)} %copy-done.1, f32[4,512]{1,0:T(4,128)S(1)} %copy-done.14, pred[512,2048]{1,0:T(8,128)(4,1)S(1)} %broadcast_and_fusion.1, f32[512,4]{0,1:T(4,128)S(1)} %get-tuple-element.227), kind=kOutput, calls=%fused_computation.37 | convolution fusion | flops 553910272 | bytes 19939328 | tf_op jit(solution)/shard_map/hbk,khd->bhd/dot_general | solution.py:65
  158.0 10.0 %fusion.79 = (bf16[32,128,1,256]{3,2,1,0:T(2,128)(2,1)}, bf16[32,128,1,256]{3,2,1,0:T(2,128)(2,1)}) fusion(bf16[32,128,2,256]{3,2,1,0:T(2,128)(2,1)} %param.30), kind=kLoop, calls=%fused_computation.141 | loop fusion | bytes 8388608 | tf_op jit(solution)/shard_map/slice | solution.py:85
  168.0 9.8 %copy.105 = bf16[32,128,1,256]{1,3,0,2:T(8,128)(2,1)} copy(bf16[32,128,1,256]{3,2,1,0:T(2,128)(2,1)} %get-tuple-element.229) | data formatting | bytes 4194304
  177.8 8.6 %copy.106 = bf16[32,128,1,256]{1,3,0,2:T(8,128)(2,1)S(1)} copy(bf16[32,128,1,256]{3,2,1,0:T(2,128)(2,1)} %get-tuple-element.230) | data formatting | bytes 4194304
  186.5 2.2 fusion.56
  190.2 23.4 %all-gather = f32[8192,4]{0,1:T(4,128)S(1)} all-gather(f32[512,4]{0,1:T(4,128)S(1)} %get-tuple-element.245), channel_id=2, replica_groups=mesh['req'=16,'tp'=8] {'req'}, dimensions={0}, use_global_device_ids=true | all-gather | bytes 139264 | tf_op jit(solution)/shard_map/all_gather | solution.py:15
  213.6 21.6 %all-gather.1 = f32[8192,4]{0,1:T(4,128)S(1)} all-gather(f32[512,4]{0,1:T(4,128)S(1)} %get-tuple-element.226), channel_id=3, replica_groups=mesh['req'=16,'tp'=8] {'req'}, dimensions={0}, use_global_device_ids=true | all-gather | bytes 139264 | tf_op jit(solution)/shard_map/all_gather | solution.py:15
  236.5 23.7 %while.19 = (s32[]{:T(128)}, f32[512,4]{0,1:T(4,128)S(1)}, f32[512,4]{0,1:T(4,128)S(1)}, f32[512,256]{0,1:T(8,128)S(1)}, f32[16,512,4]{1,2,0:T(4,128)S(1)}, /*in...) while((s32[]{:T(128)}, f32[512,4]{0,1:T(4,128)S(1)}, ...), condition=%wide.region_12.13_spmd, body=%wide.region_11.12_spmd.sunk | while | flops 405509 | bytes 3752087 | solution.py:21
  262.7 10.1 %copy.110 = bf16[256,8,2,1024]{3,1,2,0:T(8,128)(2,1)} copy(bf16[256,8,2,1024]{3,2,1,0:T(2,128)(2,1)} %bitcast.183) | data formatting | bytes 16777216
  272.8 12.5 %copy.91 = bf16[2048,2048]{1,0:T(8,128)(2,1)} copy(bf16[2048,2048]{0,1:T(8,128)(2,1)} %bitcast.182) | data formatting | bytes 16777216 | tf_op jit(solution)/shard_map/dot_general | solution.py:236
  285.3 3.0 all-gather.11.cloned.1.call-done
  290.2 6.1 %fusion.40 = f32[32,2,1024]{2,0,1:T(8,128)S(1)} fusion(bf16[2,1024,2048]{2,1,0:T(8,128)(2,1)} %bitcast.181, f32[32,2048]{1,0:T(8,128)S(1)} %get-tuple-element.219, f32[2048]{0:T(1024)S(1)} %convert_element_type.94, f32[32]{0:T(128)S(1)} %add_rsqrt_fusion.1), kind=kOutput, calls=%fused_computation.56 | convolution fusion | flops 268632064 | bytes 8921216 | tf_op jit(solution)/shard_map/dot_general | solution.py:236
  297.9 31.3 %reduce-scatter.2.cloned.1.call-done = f32[32,256]{1,0:T(8,128)} async-done(((f32[32,2048]{1,0:T(8,128)}), f32[32,256]{1,0:T(8,128)}) %reduce-scatter.2.cloned.1.call-update) | async-done | bytes 32784 | tf_op jit(solution)/shard_map/reduce_scatter | solution.py:240
  (185 shorter events, 62.2 us)
Async XLA Ops:
  6.5 255.1 %copy-start = (bf16[256,2048]{1,0:T(8,128)(2,1)S(1)}, bf16[256,2048]{1,0:T(8,128)(2,1)}, u32[]{:S(2)}) copy-start(bf16[256,2048]{1,0:T(8,128)(2,1)} %param.25) | copy-start | bytes 3145732
  6.5 89.2 %all-gather.7.cloned.1.call-start = ((), (), s32[]{:S(2)}) async-start(), calls=%async_computation.1 | async-start | bytes 1179648 | tf_op jit(solution)/shard_map/all_gather | solution.py:150
  7.3 228.0 %all-gather.9.cloned.1.call-start = ((), (), s32[]{:S(2)}) async-start(), calls=%async_computation.2 | async-start | bytes 8912896 | tf_op jit(solution)/shard_map/all_gather | solution.py:15
  16.6 4.6 %copy-start.7 = (bf16[32,2048]{1,0:T(8,128)(2,1)S(1)}, bf16[32,2048]{1,0:T(8,128)(2,1)}, u32[]{:S(2)}) copy-start(bf16[32,2048]{1,0:T(8,128)(2,1)} %param.20) | copy-start | bytes 393220
  18.7 5.4 %copy-start.21 = (s32[8]{0:T(128)S(1)}, s32[8]{0:T(128)}, u32[]{:S(2)}) copy-start(s32[8]{0:T(128)} %param.33) | copy-start | bytes 100
  18.7 5.5 %copy-start.19 = (s32[32]{0:T(128)S(1)}, s32[32]{0:T(128)}, u32[]{:S(2)}) copy-start(s32[32]{0:T(128)} %param.35) | copy-start | bytes 388
  21.2 33.4 %copy-start.3 = (bf16[8,256,2,256]{3,2,1,0:T(2,128)(2,1)S(1)}, bf16[8,256,2,256]{3,2,1,0:T(2,128)(2,1)}, u32[]{:S(2)}) copy-start(bf16[8,256,2,256]{3,2,1,0:T(2,128)(2,1)} %param.28) | copy-start | bytes 6291460
  24.1 0.7 copy-start.9
  25.5 0.6 copy-start.11
  54.6 11.5 %copy-start.18 = (s32[1,256]{1,0:T(1,128)S(1)}, s32[1,256]{1,0:T(1,128)}, u32[]{:S(2)}) copy-start(s32[1,256]{1,0:T(1,128)} %param.32) | copy-start | bytes 3076
  58.8 12.8 %copy-start.4 = (bf16[2048,1,256]{2,1,0:T(2,128)(2,1)S(1)}, bf16[2048,1,256]{2,1,0:T(2,128)(2,1)}, u32[]{:S(2)}) copy-start(bf16[2048,1,256]{2,1,0:T(2,128)(2,1)} %get-tuple-element.233) | copy-start | bytes 3145732
  75.9 4.5 %copy-start.5 = (bf16[2048,1,256]{0,2,1:T(8,128)(2,1)S(1)}, bf16[2048,1,256]{0,2,1:T(8,128)(2,1)}, u32[]{:S(2)}) copy-start(bf16[2048,1,256]{0,2,1:T(8,128)(2,1)} %copy.103) | copy-start | bytes 3145732
  84.9 5.7 %copy-start.1 = (f32[4,512,2048]{2,1,0:T(8,128)}, f32[4,512,2048]{2,1,0:T(8,128)S(1)}, u32[]{:S(2)}) copy-start(f32[4,512,2048]{2,1,0:T(8,128)S(1)} %get-tuple-element.253) | copy-start | bytes 50331652
  84.9 5.7 %copy-start.13 = (f32[4,512]{1,0:T(4,128)}, f32[4,512]{1,0:T(4,128)S(1)}, u32[]{:S(2)}) copy-start(f32[4,512]{1,0:T(4,128)S(1)} %get-tuple-element.252) | copy-start | bytes 24580
  95.8 4.3 %copy-start.10 = (f32[256,32]{0,1:T(8,128)S(1)}, f32[256,32]{0,1:T(8,128)}, u32[]{:S(2)}) copy-start(f32[256,32]{0,1:T(8,128)} %get-tuple-element.247) | copy-start | bytes 98308
  130.7 5.6 %copy-start.2 = (pred[512,2304]{1,0:T(8,128)(4,1)S(1)}, pred[512,2304]{1,0:T(8,128)(4,1)}, u32[]{:S(2)}) copy-start(pred[512,2304]{1,0:T(8,128)(4,1)} %pad_add_fusion) | copy-start | bytes 3538948
  136.4 5.1 %copy-start.14 = (f32[4,512]{1,0:T(4,128)S(1)}, f32[4,512]{1,0:T(4,128)}, u32[]{:S(2)}) copy-start(f32[4,512]{1,0:T(4,128)} %copy-done.13) | copy-start | bytes 24580
  136.4 5.1 %copy-start.15 = (f32[4,512]{1,0:T(4,128)S(1)}, f32[4,512]{1,0:T(4,128)}, u32[]{:S(2)}) copy-start(f32[4,512]{1,0:T(4,128)} %fusion.6) | copy-start | bytes 24580
  157.9 130.4 %all-gather.11.cloned.1.call-start = ((), (), s32[]{:S(2)}) async-start(), calls=%async_computation.4 | async-start | bytes 2359296 | tf_op jit(solution)/shard_map/all_gather | solution.py:229
  177.8 8.6 %copy-start.20 = (s32[32]{0:T(128)S(1)}, s32[32]{0:T(128)}, u32[]{:S(2)}) copy-start(s32[32]{0:T(128)} %param.35) | copy-start | bytes 388
  177.8 8.7 %copy-start.12 = (bf16[32,4,64]{2,0,1:T(8,128)(2,1)S(1)}, bf16[32,4,64]{2,0,1:T(8,128)(2,1)}, u32[]{:S(2)}) copy-start(bf16[32,4,64]{2,0,1:T(8,128)(2,1)} %copy-done.11) | copy-start | bytes 49156
  236.5 23.9 %copy-start.16 = (f32[32,4]{0,1:T(4,128)S(1)}, f32[32,4]{0,1:T(4,128)}, u32[]{:S(2)}) copy-start(f32[32,4]{0,1:T(4,128)} %get-tuple-element.224) | copy-start | bytes 1540
  262.7 66.5 %reduce-scatter.2.cloned.1.call-start = ((), (), s32[]{:S(2)}) async-start(), calls=%async_computation.3 | async-start | bytes 294912 | tf_op jit(solution)/shard_map/reduce_scatter | solution.py:240
  272.8 12.5 %copy-start.17 = (bf16[2048]{0:T(1024)(128)(2,1)S(1)}, bf16[2048]{0:T(1024)(128)(2,1)}, u32[]{:S(2)}) copy-start(bf16[2048]{0:T(1024)(128)(2,1)} %param.22) | copy-start | bytes 12292
  272.8 17.2 %copy-start.8 = (bf16[32,2048]{1,0:T(8,128)(2,1)S(1)}, bf16[32,2048]{1,0:T(8,128)(2,1)}, u32[]{:S(2)}) copy-start(bf16[32,2048]{1,0:T(8,128)(2,1)} %param.20) | copy-start | bytes 393220
  290.2 6.1 %copy-start.6 = (bf16[1024,2048]{1,0:T(8,128)(2,1)S(1)}, bf16[1024,2048]{1,0:T(8,128)(2,1)}, u32[]{:S(2)}) copy-start(bf16[1024,2048]{1,0:T(8,128)(2,1)} %param.27) | copy-start | bytes 12582916
Sparse Core Ops, SparseCore 0:
  9.0 26.0 all-gather.6
  158.0 71.9 all-gather.8
  262.8 25.5 all-gather.10
  298.0 31.0 reduce-scatter.1
